TPU v7x, 32 devices: a whole 2x2x4 slice. The times are simulated.
32 devices in a mesh: dp: 8 (over y, x, core), mp: 4 (over z).
Axes of the slice: x: 2, y: 2, z: 4, core: 2. Of those that a mesh axis runs over, the one named last changes fastest.
Arguments:
- factor_rows: bfloat16 [4, 8, 8, 768], P('mp', None, 'dp')
- old_statistic: float32 [8, 4, 768, 768], P('dp', 'mp'), may hold values from -1 to 2, as said below
- assignment: int32 [4, 8], P('mp'), may hold values from 0 to 7, each once within a row
- gradient: bfloat16 [8, 4, 768, 512], P('dp', None, None, 'mp'), may hold values from -3 to 3
Outputs:
- update: bfloat16 [8, 4, 768, 512], P('dp', None, None, 'mp')
Inputs may be any that keep to these rules, and one draw needn't show every extreme that they name: Each row of assignment names every block number once. `old_statistic`: each block is symmetric positive definite.
All inputs are finite; a program needn't handle non-finite values.
Results may differ from a plain program's by a relative error of at most 0.001.
The roundings to bfloat16 on the way count: a program that leaves them out, or rounds other values in their place, can miss the bound.
Values may be sent and summed in bfloat16 or wider, within the bound.
No kernel may reach another device: no remote copies, remote signals or barrier semaphores. Data moves between devices by JAX's collectives and lax.ppermute only.
A program may use at most 64 MiB of HBM per device.

v0:
```python
import jax
import jax.numpy as jnp
from jax import lax
from jax.sharding import PartitionSpec as P


def newton_factors(statistic):
    identity = jnp.eye(statistic.shape[0], dtype=jnp.float32)
    frob_norm = jnp.sqrt(jnp.sum(statistic * statistic) + 1e-06)
    normed = statistic / frob_norm
    step_one = ((5.0 * identity - normed) * 0.25).astype(jnp.bfloat16)
    square_one = jnp.dot(step_one, step_one, preferred_element_type=jnp.float32).astype(
        jnp.bfloat16
    )
    product_one = jnp.dot(
        square_one, normed.astype(jnp.bfloat16), preferred_element_type=jnp.float32
    ).astype(jnp.bfloat16)
    coupled_one = jnp.dot(square_one, product_one, preferred_element_type=jnp.float32)
    step_two = ((5.0 * identity - coupled_one) * 0.25).astype(jnp.bfloat16)
    square_two = jnp.dot(step_two, step_two, preferred_element_type=jnp.float32).astype(
        jnp.bfloat16
    )
    product_two = jnp.dot(
        square_two, coupled_one.astype(jnp.bfloat16), preferred_element_type=jnp.float32
    ).astype(jnp.bfloat16)
    coupled_two = jnp.dot(square_two, product_two, preferred_element_type=jnp.float32)
    step_three = ((5.0 * identity - coupled_two) / (4.0 * jnp.sqrt(jnp.sqrt(frob_norm)))).astype(
        jnp.bfloat16
    )
    return jnp.stack([step_one, step_two, step_three])


def body(factor_rows, old_statistic, assignment, gradient):
    chosen = assignment[0]
    picked = jnp.take(factor_rows[0], chosen, axis=0)
    arrived = lax.all_to_all(picked, "dp", split_axis=0, concat_axis=1, tiled=True)
    factors = arrived[0]
    count = factors.shape[0]
    gram = lax.dot_general(
        factors, factors, (((0,), (0,)), ((), ())), preferred_element_type=jnp.float32
    )
    statistic = old_statistic[0, 0] + gram / count
    stacked = newton_factors(statistic)
    first_pass = jnp.einsum(
        "ij,nkjc->nkic",
        stacked[2],
        lax.all_to_all(gradient, "mp", split_axis=1, concat_axis=3, tiled=True),
        preferred_element_type=jnp.float32,
    ).astype(jnp.bfloat16)
    second_pass = jnp.einsum(
        "ij,nkjc->nkic", stacked[1], first_pass, preferred_element_type=jnp.float32
    ).astype(jnp.bfloat16)
    result = jnp.einsum(
        "ij,nkjc->nkic", stacked[0], second_pass, preferred_element_type=jnp.float32
    ).astype(jnp.bfloat16)
    return lax.all_to_all(result, "mp", split_axis=3, concat_axis=1, tiled=True)


def solution(mesh):
    return jax.shard_map(
        body,
        mesh=mesh,
        in_specs=(
            P("mp", None, "dp", None),
            P("dp", "mp", None, None),
            P("mp", None),
            P("dp", None, None, "mp"),
        ),
        out_specs=P("dp", None, None, "mp"),
        check_vma=False,
    )
```

profile of v0, /device:TPU:0, one launch (start us, length us, event | category | flops | bytes accessed | tf_op | source)
XLA Modules:
  0.0 77.3 jit_solution(11541387428655440850)
XLA Ops:
  0.0 0.7 fusion.18
  0.7 0.7 compare_and_fusion
  1.4 0.6 gather_fusion
  2.0 0.5 broadcast.94
  2.5 0.6 reduce
  3.2 0.6 reshape.92
  3.8 5.2 %all-to-all-start = ((bf16[8,2,384]{2,1,0:T(2,128)(2,1)}), bf16[8,2,384]{2,1,0:T(2,128)(2,1)S(1)}, u32[]{:S(2)}, u32[]{:S(2)}) async-start(bf16[8,2,384]{2,1,0:T(2,128)(2,1)} %reshape.92), calls=%async_computation | async-start | bytes 24576 | tf_op jit(solution)/shard_map/all_to_all | solution.py:36
  9.0 2.3 %copy.13 = bf16[1,4,768,128]{2,3,0,1:T(8,128)(2,1)} copy(bf16[1,4,768,128]{3,2,1,0:T(8,128)(2,1)} %param.7) | data formatting | bytes 1572864 | tf_op args[3]
  11.3 2.4 %all-to-all-done = bf16[8,2,384]{2,1,0:T(2,128)(2,1)S(1)} async-done(((bf16[8,2,384]{2,1,0:T(2,128)(2,1)}), bf16[8,2,384]{2,1,0:T(2,128)(2,1)S(1)}, u32[]{:S(2)}, u32[]{:S(2)}) %all-to-all-start) | async-done | bytes 12320 | tf_op jit(solution)/shard_map/all_to_all | solution.py:36
  13.7 4.9 %all-to-all-start.1 = ((bf16[1,4,768,128]{2,3,0,1:T(8,128)(2,1)}), bf16[1,4,768,128]{2,3,0,1:T(8,128)(2,1)}, u32[]{:S(2)}, u32[]{:S(2)}) async-start(bf16[1,4,768,128]{2,3,0,1:T(8,128)(2,1)} %copy.13), calls=%async_computation.1 | async-start | bytes 1572864 | tf_op jit(solution)/shard_map/all_to_all | solution.py:47
  18.6 3.2 %multiply_reduce_fusion = (f32[]{:T(128)}, f32[768,768]{1,0:T(8,128)S(1)}) fusion(bf16[8,1,768]{2,1,0:T(2,128)(2,1)S(1)} %reshape.93, f32[1,1,768,768]{3,2,1,0:T(8,128)} %param.5), kind=kOutput, calls=%fused_computation.11 | convolution fusion | flops 11796479 | bytes 4730884 | tf_op jit(solution)/shard_map/dot_general | solution.py:39
  22.5 0.3 fusion.1
  22.9 2.1 %convolution_convert_fusion.3 = bf16[768,768]{1,0:T(8,128)(2,1)} fusion(bf16[768,768]{1,0:T(8,128)(2,1)S(1)} %fusion.1), kind=kOutput, calls=%fused_computation.16 | convolution fusion | flops 906559488 | bytes 2359296 | tf_op jit(solution)/shard_map/dot_general | solution.py:12
  25.0 5.1 %fusion.11 = f32[768,768]{1,0:T(8,128)} fusion(bf16[768,768]{1,0:T(8,128)(2,1)} %convolution_convert_fusion.3, f32[768,768]{1,0:T(8,128)S(1)} %get-tuple-element.6, f32[]{:T(128)S(6)} %sqrt.9), kind=kOutput, calls=%fused_computation.25 | convolution fusion | flops 1813708800 | bytes 5898244 | tf_op jit(solution)/shard_map/dot_general | solution.py:18
  30.1 3.6 %convolution_convert_fusion.1 = bf16[768,768]{1,0:T(8,128)(2,1)S(1)} fusion(f32[768,768]{1,0:T(8,128)} %fusion.11), kind=kOutput, calls=%fused_computation.14 | convolution fusion | flops 909508608 | bytes 3538944 | tf_op jit(solution)/shard_map/dot_general | solution.py:20
  33.8 1.1 %convolution_convert_fusion = bf16[768,768]{1,0:T(8,128)(2,1)S(1)} fusion(bf16[768,768]{1,0:T(8,128)(2,1)S(1)} %convolution_convert_fusion.1, f32[768,768]{1,0:T(8,128)S(1)} %copy-done.1), kind=kOutput, calls=%fused_computation.13 | convolution fusion | flops 907149312 | bytes 4718592 | tf_op jit(solution)/shard_map/dot_general | solution.py:23
  34.9 3.9 %all-to-all-done.1 = bf16[1,4,768,128]{2,3,0,1:T(8,128)(2,1)} async-done(((bf16[1,4,768,128]{2,3,0,1:T(8,128)(2,1)}), bf16[1,4,768,128]{2,3,0,1:T(8,128)(2,1)}, u32[]{:S(2)}, u32[]{:S(2)}) %all-to-all-start.1) | async-done | bytes 786464 | tf_op jit(solution)/shard_map/all_to_all | solution.py:47
  38.7 3.7 %convolution_convert_fusion.6 = bf16[768,512]{1,0:T(8,128)(2,1)} fusion(bf16[768,512]{0,1:T(8,128)(2,1)} %bitcast.8, bf16[768,768]{1,0:T(8,128)(2,1)S(1)} %convolution_convert_fusion.1, bf16[768,768]{1,0:T(8,128)(2,1)S(1)} %convolution_convert_fusion, f32[]{:T(128)S(6)} %mul_shard_map.3), kind=kOutput, calls=%fused_computation.19 | convolution fusion | flops 1513291776 | bytes 3932164 | tf_op jit(solution)/shard_map/ij,nkjc->nkic/dot_general | solution.py:44
  42.5 3.5 %fusion.7 = bf16[1,1,768,512]{2,3,1,0:T(8,128)(2,1)S(1)} fusion(bf16[768,768]{1,0:T(8,128)(2,1)S(1)} %fusion.1, bf16[768,512]{1,0:T(8,128)(2,1)} %convolution_convert_fusion.6, f32[768,768]{1,0:T(8,128)} %fusion.11), kind=kOutput, calls=%fused_computation.21 | convolution fusion | flops 1211695104 | bytes 5111808 | tf_op jit(solution)/shard_map/ij,nkjc->nkic/dot_general | solution.py:53
  45.9 1.2 %copy.25 = bf16[1,1,768,512]{2,1,0,3:T(2,128)(2,1)S(1)} copy(bf16[1,1,768,512]{2,3,1,0:T(8,128)(2,1)S(1)} %fusion.7) | data formatting | bytes 1572864 | tf_op jit(solution)/shard_map/convert_element_type | solution.py:55
  47.1 5.8 %reduce.1 = bf16[512,768]{1,0:T(8,128)(2,1)S(1)} reduce(bf16[512,1,1,768]{3,2,1,0:T(2,128)(2,1)S(1)} %bitcast.60, bf16[]{:T(256)} %broadcast.94), dimensions={1,2}, to_apply=%bitcast.58.reduce_sub_computation | reduce | bytes 1572866
  53.1 22.1 %all_to_all.42 = bf16[4,2,49152]{2,1,0:T(2,128)(2,1)S(1)} all-to-all(bf16[4,2,49152]{2,1,0:T(2,128)(2,1)S(1)} %reshape.94), channel_id=1, replica_groups=mesh['dp'=8,'mp'=4] {'mp'}, dimensions={0} | all-to-all | bytes 1572864 | tf_op jit(solution)/shard_map/all_to_all | solution.py:56
  75.2 0.7 reshape.95
  76.1 1.2 %copy.15 = bf16[1,4,768,128]{3,2,1,0:T(8,128)(2,1)} copy(bf16[1,4,768,128]{2,3,1,0:T(8,128)(2,1)S(1)} %bitcast.62) | data formatting | bytes 1572864 | tf_op jit(solution)/shard_map/all_to_all | solution.py:56
  (9 shorter events, 0.4 us)
Async XLA Ops:
  0.0 1.3 %copy-start = (bf16[1,8,1,768]{3,1,2,0:T(8,128)(2,1)S(1)}, bf16[1,8,1,768]{3,1,2,0:T(8,128)(2,1)}, u32[]{:S(2)}) copy-start(bf16[1,8,1,768]{3,1,2,0:T(8,128)(2,1)} %param.4) | copy-start | bytes 36868
  3.8 9.9 %all-to-all-start = ((bf16[8,2,384]{2,1,0:T(2,128)(2,1)}), bf16[8,2,384]{2,1,0:T(2,128)(2,1)S(1)}, u32[]{:S(2)}, u32[]{:S(2)}) async-start(bf16[8,2,384]{2,1,0:T(2,128)(2,1)} %reshape.92), calls=%async_computation | async-start | bytes 24576 | tf_op jit(solution)/shard_map/all_to_all | solution.py:36
  13.7 25.0 %all-to-all-start.1 = ((bf16[1,4,768,128]{2,3,0,1:T(8,128)(2,1)}), bf16[1,4,768,128]{2,3,0,1:T(8,128)(2,1)}, u32[]{:S(2)}, u32[]{:S(2)}) async-start(bf16[1,4,768,128]{2,3,0,1:T(8,128)(2,1)} %copy.13), calls=%async_computation.1 | async-start | bytes 1572864 | tf_op jit(solution)/shard_map/all_to_all | solution.py:47
  30.1 3.7 %copy-start.1 = (f32[768,768]{1,0:T(8,128)S(1)}, f32[768,768]{1,0:T(8,128)}, u32[]{:S(2)}) copy-start(f32[768,768]{1,0:T(8,128)} %fusion.11) | copy-start | bytes 7077892
where the time goes:
time: 77.8 us; the launch traced here: 77.3 us
  matrix products  22.3 us (29%)
  blocking collectives  22.1 us (28%)
  starting transfers between devices  10.1 us (13%)
  other arithmetic  8.12 us (10%)
  local copies, waits for them, and re-layouts  7.49 us (10%)
  waiting for transfers between devices  6.3 us (8%)
  between operations  0.93 us (1%)
    all_to_all x1, blocking collectives, body(): return lax.all_to_all(result, 'mp', split_axis=3, concat_axis=1, tiled=True)  22.1 us
    unnamed x1, other arithmetic  5.77 us
    all_to_all x1, starting transfers between devices, body(): lax.all_to_all(picked, 'dp', split_axis=0, concat_axis=1, tiled=True)  5.2 us
    dot_general x1, matrix products, newton_factors(): jnp.dot(square_one, product_one, preferred_element_type=jnp.float32)  5.06 us
    all_to_all x1, starting transfers between devices, body(): lax.all_to_all(gradient, 'mp', split_axis=1, concat_axis=3, tiled=True)  4.87 us
    unnamed x10, local copies, waits for them, and re-layouts  4 us
    all_to_all x1, waiting for transfers between devices, body(): lax.all_to_all(gradient, 'mp', split_axis=1, concat_axis=3, tiled=True)  3.85 us
    dot_general x1, matrix products, body(): jnp.einsum('ij,nkjc->nkic', stacked[2], lax.all_to_all(gradient, 'mp', sp...  3.71 us
  transfers between devices with their start and end apart: 2, of which 2 were waited for; matrix products, arithmetic and copies ran while one was open for 23% of the time, Pallas kernels for 0%

commit v1 on v0

--- a/solution.py
+++ b/solution.py
@@ -2,6 +2,12 @@
 import jax.numpy as jnp
 from jax import lax
 from jax.sharding import PartitionSpec as P
+
+
+def exchange_blocks(x, axis, split, join):
+    pieces = jnp.split(x, lax.axis_size(axis), axis=split)
+    received = lax.all_to_all(jnp.stack(pieces), axis, 0, 0)
+    return jnp.concatenate(received, axis=join)
 
 
 def newton_factors(statistic):
@@ -53,7 +59,7 @@
     result = jnp.einsum(
         "ij,nkjc->nkic", stacked[0], second_pass, preferred_element_type=jnp.float32
     ).astype(jnp.bfloat16)
-    return lax.all_to_all(result, "mp", split_axis=3, concat_axis=1, tiled=True)
+    return exchange_blocks(result, "mp", 3, 1)
 
 
 def solution(mesh):

time: 77.8 us -> 69.8 us (0.90)
  other arithmetic: 8.12 us -> 2.49 us
  local copies, waits for them, and re-layouts: 7.49 us -> 5.21 us
    unnamed x1 -> x0, other arithmetic: 5.77 us -> none
    convert_element_type x1 -> x0, local copies, waits for them, and re-layouts: 1.21 us -> none  [body(): result = jnp.einsum('ij,nkjc->nkic', stacked[0], second_pass, preferred_e...]
    all_to_all x1 -> x0, local copies, waits for them, and re-layouts: 1.15 us -> none  [body(): return lax.all_to_all(result, 'mp', split_axis=3, concat_axis=1, tiled=True)]
    reshape x0 -> x1, local copies, waits for them, and re-layouts: none -> 1.15 us  [exchange_blocks(): return jnp.concatenate(received, axis=join)]
    unnamed x10 -> x7, local copies, waits for them, and re-layouts: 4 us -> 2.92 us
  transfers between devices with their start and end apart: 2 -> 2, of which waited for: 2 -> 2; matrix products, arithmetic and copies ran while one was open for 23% -> 26% of each run, Pallas kernels for 0% -> 0%
where the time goes in v1:
time: 69.8 us; the launch traced here: 69.3 us
  matrix products  22.2 us (32%)
  blocking collectives  22.1 us (32%)
  starting transfers between devices  10.1 us (14%)
  waiting for transfers between devices  6.38 us (9%)
  local copies, waits for them, and re-layouts  5.21 us (7%)
  other arithmetic  2.49 us (4%)
  between operations  0.85 us (1%)
    all_to_all x1, blocking collectives, exchange_blocks(): received = lax.all_to_all(jnp.stack(pieces), axis, 0, 0)  22.1 us
    all_to_all x1, starting transfers between devices, body(): lax.all_to_all(picked, 'dp', split_axis=0, concat_axis=1, tiled=True)  5.2 us
    dot_general x1, matrix products, newton_factors(): jnp.dot(square_one, product_one, preferred_element_type=jnp.float32)  5.06 us
    all_to_all x1, starting transfers between devices, body(): lax.all_to_all(gradient, 'mp', split_axis=1, concat_axis=3, tiled=True)  4.87 us
    all_to_all x1, waiting for transfers between devices, body(): lax.all_to_all(gradient, 'mp', split_axis=1, concat_axis=3, tiled=True)  3.94 us
    dot_general x1, matrix products, body(): jnp.einsum('ij,nkjc->nkic', stacked[2], lax.all_to_all(gradient, 'mp', sp...  3.71 us
    dot_general x1, matrix products, newton_factors(): jnp.dot(step_two, step_two, preferred_element_type=jnp.float32)  3.65 us
    dot_general x1, matrix products, body(): jnp.einsum('ij,nkjc->nkic', stacked[0], second_pass, preferred_element_ty...  3.45 us
  transfers between devices with their start and end apart: 2, of which 2 were waited for; matrix products, arithmetic and copies ran while one was open for 26% of the time, Pallas kernels for 0%

profile of v1, /device:TPU:0, one launch (start us, length us, event | category | flops | bytes accessed | tf_op | source)
XLA Modules:
  0.0 69.3 jit_solution(7458778333132570373)
XLA Ops:
  0.0 0.7 fusion.18
  0.7 0.7 compare_and_fusion
  1.4 0.6 gather_fusion
  1.9 0.1 bitcast_select_fusion
  2.0 0.5 broadcast.94
  2.5 0.6 reduce
  3.2 0.6 reshape.96
  3.8 5.2 %all-to-all-start = ((bf16[8,2,384]{2,1,0:T(2,128)(2,1)}), bf16[8,2,384]{2,1,0:T(2,128)(2,1)S(1)}, u32[]{:S(2)}, u32[]{:S(2)}) async-start(bf16[8,2,384]{2,1,0:T(2,128)(2,1)} %reshape.96), calls=%async_computation | async-start | bytes 24576 | tf_op jit(solution)/shard_map/all_to_all | solution.py:42
  9.0 2.3 %copy.12 = bf16[1,4,768,128]{2,3,0,1:T(8,128)(2,1)} copy(bf16[1,4,768,128]{3,2,1,0:T(8,128)(2,1)} %param.7) | data formatting | bytes 1572864 | tf_op args[3]
  11.3 2.4 %all-to-all-done = bf16[8,2,384]{2,1,0:T(2,128)(2,1)S(1)} async-done(((bf16[8,2,384]{2,1,0:T(2,128)(2,1)}), bf16[8,2,384]{2,1,0:T(2,128)(2,1)S(1)}, u32[]{:S(2)}, u32[]{:S(2)}) %all-to-all-start) | async-done | bytes 12320 | tf_op jit(solution)/shard_map/all_to_all | solution.py:42
  13.7 4.9 %all-to-all-start.1 = ((bf16[1,4,768,128]{2,3,0,1:T(8,128)(2,1)}), bf16[1,4,768,128]{2,3,0,1:T(8,128)(2,1)}, u32[]{:S(2)}, u32[]{:S(2)}) async-start(bf16[1,4,768,128]{2,3,0,1:T(8,128)(2,1)} %copy.12), calls=%async_computation.1 | async-start | bytes 1572864 | tf_op jit(solution)/shard_map/all_to_all | solution.py:53
  18.6 3.2 %multiply_reduce_fusion = (f32[]{:T(128)}, f32[768,768]{1,0:T(8,128)S(1)}) fusion(bf16[8,1,768]{2,1,0:T(2,128)(2,1)S(1)} %reshape.97, f32[1,1,768,768]{3,2,1,0:T(8,128)} %param.5), kind=kOutput, calls=%fused_computation.11 | convolution fusion | flops 11796479 | bytes 4730884 | tf_op jit(solution)/shard_map/dot_general | solution.py:45
  22.5 0.3 fusion.1
  22.8 2.1 %convolution_convert_fusion.3 = bf16[768,768]{1,0:T(8,128)(2,1)} fusion(bf16[768,768]{1,0:T(8,128)(2,1)S(1)} %fusion.1), kind=kOutput, calls=%fused_computation.16 | convolution fusion | flops 906559488 | bytes 2359296 | tf_op jit(solution)/shard_map/dot_general | solution.py:18
  25.0 5.1 %fusion.11 = f32[768,768]{1,0:T(8,128)} fusion(bf16[768,768]{1,0:T(8,128)(2,1)} %convolution_convert_fusion.3, f32[768,768]{1,0:T(8,128)S(1)} %get-tuple-element.10, f32[]{:T(128)S(6)} %sqrt.9), kind=kOutput, calls=%fused_computation.25 | convolution fusion | flops 1813708800 | bytes 5898244 | tf_op jit(solution)/shard_map/dot_general | solution.py:24
  30.0 3.6 %convolution_convert_fusion.1 = bf16[768,768]{1,0:T(8,128)(2,1)S(1)} fusion(f32[768,768]{1,0:T(8,128)} %fusion.11), kind=kOutput, calls=%fused_computation.14 | convolution fusion | flops 909508608 | bytes 3538944 | tf_op jit(solution)/shard_map/dot_general | solution.py:26
  33.7 1.1 %convolution_convert_fusion = bf16[768,768]{1,0:T(8,128)(2,1)S(1)} fusion(bf16[768,768]{1,0:T(8,128)(2,1)S(1)} %convolution_convert_fusion.1, f32[768,768]{1,0:T(8,128)S(1)} %copy-done.1), kind=kOutput, calls=%fused_computation.13 | convolution fusion | flops 907149312 | bytes 4718592 | tf_op jit(solution)/shard_map/dot_general | solution.py:29
  34.8 3.9 %all-to-all-done.1 = bf16[1,4,768,128]{2,3,0,1:T(8,128)(2,1)} async-done(((bf16[1,4,768,128]{2,3,0,1:T(8,128)(2,1)}), bf16[1,4,768,128]{2,3,0,1:T(8,128)(2,1)}, u32[]{:S(2)}, u32[]{:S(2)}) %all-to-all-start.1) | async-done | bytes 786464 | tf_op jit(solution)/shard_map/all_to_all | solution.py:53
  38.8 3.7 %convolution_convert_fusion.6 = bf16[768,512]{1,0:T(8,128)(2,1)} fusion(bf16[768,512]{0,1:T(8,128)(2,1)} %bitcast.8, bf16[768,768]{1,0:T(8,128)(2,1)S(1)} %convolution_convert_fusion.1, bf16[768,768]{1,0:T(8,128)(2,1)S(1)} %convolution_convert_fusion, f32[]{:T(128)S(6)} %mul_shard_map.3), kind=kOutput, calls=%fused_computation.19 | convolution fusion | flops 1513291776 | bytes 3932164 | tf_op jit(solution)/shard_map/ij,nkjc->nkic/dot_general | solution.py:50
  42.5 3.5 %fusion.7 = bf16[1,1,768,512]{2,3,1,0:T(8,128)(2,1)S(1)} fusion(bf16[768,768]{1,0:T(8,128)(2,1)S(1)} %fusion.1, bf16[768,512]{1,0:T(8,128)(2,1)} %convolution_convert_fusion.6, f32[768,768]{1,0:T(8,128)} %fusion.11), kind=kOutput, calls=%fused_computation.21 | convolution fusion | flops 1211695104 | bytes 5111808 | tf_op jit(solution)/shard_map/ij,nkjc->nkic/dot_general | solution.py:59
  45.9 0.1 slice_bitcast_fusion.3
  46.0 0.1 pad_maximum_fusion
  46.1 22.1 %all_to_all.29 = bf16[4,1,1,768,128]{3,4,2,1,0:T(8,128)(2,1)S(1)} all-to-all(bf16[4,1,1,768,128]{3,4,2,1,0:T(8,128)(2,1)S(1)} %pad_maximum_fusion), channel_id=1, replica_groups=mesh['dp'=8,'mp'=4] {'mp'}, dimensions={0} | all-to-all | bytes 1572864 | tf_op jit(solution)/shard_map/all_to_all | solution.py:9
  68.2 1.2 %copy.13 = bf16[1,4,768,128]{3,2,1,0:T(8,128)(2,1)} copy(bf16[1,4,768,128]{2,3,1,0:T(8,128)(2,1)S(1)} %bitcast.60) | data formatting | bytes 1572864 | tf_op jit(solution)/shard_map/reshape | solution.py:10
  (6 shorter events, 0.0 us)
Async XLA Ops:
  0.0 1.3 %copy-start = (bf16[1,8,1,768]{3,1,2,0:T(8,128)(2,1)S(1)}, bf16[1,8,1,768]{3,1,2,0:T(8,128)(2,1)}, u32[]{:S(2)}) copy-start(bf16[1,8,1,768]{3,1,2,0:T(8,128)(2,1)} %param.4) | copy-start | bytes 36868
  3.8 9.9 %all-to-all-start = ((bf16[8,2,384]{2,1,0:T(2,128)(2,1)}), bf16[8,2,384]{2,1,0:T(2,128)(2,1)S(1)}, u32[]{:S(2)}, u32[]{:S(2)}) async-start(bf16[8,2,384]{2,1,0:T(2,128)(2,1)} %reshape.96), calls=%async_computation | async-start | bytes 24576 | tf_op jit(solution)/shard_map/all_to_all | solution.py:42
  13.7 25.0 %all-to-all-start.1 = ((bf16[1,4,768,128]{2,3,0,1:T(8,128)(2,1)}), bf16[1,4,768,128]{2,3,0,1:T(8,128)(2,1)}, u32[]{:S(2)}, u32[]{:S(2)}) async-start(bf16[1,4,768,128]{2,3,0,1:T(8,128)(2,1)} %copy.12), calls=%async_computation.1 | async-start | bytes 1572864 | tf_op jit(solution)/shard_map/all_to_all | solution.py:53
  30.0 3.7 %copy-start.1 = (f32[768,768]{1,0:T(8,128)S(1)}, f32[768,768]{1,0:T(8,128)}, u32[]{:S(2)}) copy-start(f32[768,768]{1,0:T(8,128)} %fusion.11) | copy-start | bytes 7077892
